TPU v7x, 128 devices: a whole 4x4x4 slice. The times are simulated.
128 devices in a mesh: lon: 32 (over x_hi, z, y), ch: 4 (over x_lo, core).
Axes of the slice: x: 4 (x_hi: 2, x_lo: 2; x = x_hi * 2 + x_lo), y: 4, z: 4, core: 2. Of those that a mesh axis runs over, the one named last changes fastest.
Arguments:
- ocean_state: bfloat16 [400, 64, 4096], P('ch', None, 'lon'), may hold values from -6 to 6
- sea_mask: int32 [64, 4096], P(None, 'lon'), may hold values 0 or 1
- kernel: float32 [400, 49], P('ch'), may hold values from -0.875 to 0.875
- conv_bias: float32 [400], P('ch'), may hold values from -3 to 3
- norm_gain: float32 [400], replicated, may hold values from 0.1 to 1.9
- norm_bias: float32 [400], replicated, may hold values from -2 to 2
- weight_in: bfloat16 [400, 1600], replicated, may hold values from -0.3125 to 0.3125
- bias_in: float32 [1600], replicated, may hold values from -3 to 3
- weight_out: bfloat16 [1600, 400], replicated, may hold values from -0.15625 to 0.15625
- bias_out: float32 [400], replicated, may hold values from -3 to 3
- layer_scale: float32 [400], P('ch'), may hold values from 0.5 to 2
- cotangent: bfloat16 [400, 64, 4096], P('ch', None, 'lon'), may hold values from -6 to 6
Outputs:
- updated: bfloat16 [400, 64, 4096], P('ch', None, 'lon')
- grad_state: bfloat16 [400, 64, 4096], P('ch', None, 'lon')
- grad_weight_in: float32 [400, 1600], replicated
- grad_weight_out: float32 [1600, 400], replicated
Inputs may be any that keep to these rules, and one draw needn't show every extreme that they name: `sea_mask`: 1 marks an ocean cell, 0 a land cell.
All inputs are finite; a program needn't handle non-finite values. No bound on the sum of `sea_mask` on one device may be relied on, other than what follows from the above.
Results may differ from a plain program's by a relative error of at most 0.0077.
Values may be sent and summed in bfloat16 or wider, within the bound.
No kernel may reach another device: no remote copies, remote signals or barrier semaphores. Data moves between devices by JAX's collectives and lax.ppermute only.
A program may use at most 192 MiB of HBM per device.

v0:
```python
import math
import jax
import jax.numpy as jnp
from jax import lax
from jax.sharding import PartitionSpec as P

KW = 7
root_coef = math.sqrt(2.0 / math.pi)
cubic_coef = 0.044715
norm_eps = 1e-06


def extended(cells, sides, width):
    for axis, dim in sides:
        count = lax.axis_size(axis)
        head = lax.slice_in_dim(cells, 0, width, axis=dim)
        tail = lax.slice_in_dim(cells, cells.shape[dim] - width, cells.shape[dim], axis=dim)
        cells = jnp.concatenate(
            [
                lax.ppermute(tail, axis, [(i, (i + 1) % count) for i in range(count)]),
                cells,
                lax.ppermute(head, axis, [((i + 1) % count, i) for i in range(count)]),
            ],
            axis=dim,
        )
    return cells


def gelu_parts(pre_act):
    inner_arg = root_coef * (pre_act + cubic_coef * pre_act * pre_act * pre_act)
    tangent = jnp.tanh(inner_arg)
    gelu_value = 0.5 * pre_act * (1.0 + tangent)
    gelu_slope = 0.5 * (1.0 + tangent) + 0.5 * pre_act * (1.0 - tangent * tangent) * root_coef * (
        1.0 + 3.0 * cubic_coef * pre_act * pre_act
    )
    return (gelu_value, gelu_slope)


def depth_taps(padded, kernel, row_count, lon_cells):
    tap_total = jnp.zeros((padded.shape[0], row_count, lon_cells), jnp.float32)
    for row_off in range(KW):
        for col_off in range(KW):
            tap_total = (
                tap_total
                + kernel[:, row_off * KW + col_off][:, None, None]
                * padded[:, row_off : row_off + row_count, col_off : col_off + lon_cells]
            )
    return tap_total


def depth_back(padded_grad, kernel, row_count, lon_cells):
    span = KW - 1
    tap_total = jnp.zeros((padded_grad.shape[0], row_count, lon_cells), jnp.float32)
    for row_off in range(KW):
        for col_off in range(KW):
            tap_total = (
                tap_total
                + kernel[:, row_off * KW + col_off][:, None, None]
                * padded_grad[
                    :,
                    span - row_off : span - row_off + row_count,
                    span - col_off : span - col_off + lon_cells,
                ]
            )
    return tap_total


def block_math(
    conv_cells, grad_cells, norm_gain, norm_bias, weight_in, bias_in, weight_out, bias_out
):
    full_width = conv_cells.shape[0]
    values = conv_cells.astype(jnp.float32)
    mean_val = jnp.sum(values, axis=0) / full_width
    square = jnp.sum(values * values, axis=0) / full_width
    inv_std = lax.rsqrt(square - mean_val * mean_val + norm_eps)
    centred = (values - mean_val) * inv_std
    normed = (centred * norm_gain[:, None] + norm_bias[:, None]).astype(jnp.bfloat16)
    pre_act = jnp.dot(weight_in.T, normed, preferred_element_type=jnp.float32) + bias_in[:, None]
    gelu_value, gelu_slope = gelu_parts(pre_act)
    activation = gelu_value.astype(jnp.bfloat16)
    branch = (
        jnp.dot(weight_out.T, activation, preferred_element_type=jnp.float32) + bias_out[:, None]
    ).astype(jnp.bfloat16)
    grad_act = jnp.dot(weight_out, grad_cells, preferred_element_type=jnp.float32)
    grad_pre = (grad_act * gelu_slope).astype(jnp.bfloat16)
    part_out = jnp.dot(activation, grad_cells.T, preferred_element_type=jnp.float32)
    part_in = jnp.dot(normed, grad_pre.T, preferred_element_type=jnp.float32)
    grad_normed = jnp.dot(weight_in, grad_pre, preferred_element_type=jnp.float32)
    scaled_grad = grad_normed * norm_gain[:, None]
    mean_first = jnp.sum(scaled_grad, axis=0) / full_width
    mean_second = jnp.sum(scaled_grad * centred, axis=0) / full_width
    grad_conv = (inv_std * (scaled_grad - mean_first - centred * mean_second)).astype(jnp.bfloat16)
    return (branch, grad_conv, part_in, part_out)


def body(
    ocean_state,
    sea_mask,
    kernel,
    conv_bias,
    norm_gain,
    norm_bias,
    weight_in,
    bias_in,
    weight_out,
    bias_out,
    layer_scale,
    cotangent,
):
    local_chan, row_count, lon_cells = ocean_state.shape
    chan_groups = lax.axis_size("ch")
    full_width = local_chan * chan_groups
    rim_width = KW // 2
    grad_scale = 1.0 / math.sqrt(row_count * lon_cells * lax.axis_size("lon"))
    state_f = ocean_state.astype(jnp.float32)
    state_rim = extended(ocean_state, (("lon", 2),), rim_width)
    padded = jnp.pad(state_rim.astype(jnp.float32), ((0, 0), (rim_width, rim_width), (0, 0)))
    conv_out = (depth_taps(padded, kernel, row_count, lon_cells) + conv_bias[:, None, None]).astype(
        jnp.bfloat16
    )
    mask_f = sea_mask.astype(jnp.float32)[None]
    grad_out = cotangent.astype(jnp.float32) * mask_f
    grad_branch = (grad_out * layer_scale[:, None, None]).astype(jnp.bfloat16)
    quarter = row_count // chan_groups
    conv_cells, grad_cells = (
        lax.all_to_all(conv_out, "ch", split_axis=1, concat_axis=0, tiled=True),
        lax.all_to_all(grad_branch, "ch", split_axis=1, concat_axis=0, tiled=True),
    )
    branch_cells, conv_grad_cells, part_in, part_out = block_math(
        conv_cells.reshape(full_width, quarter * lon_cells),
        grad_cells.reshape(full_width, quarter * lon_cells),
        norm_gain,
        norm_bias,
        weight_in,
        bias_in,
        weight_out,
        bias_out,
    )
    branch, grad_conv = (
        lax.all_to_all(
            branch_cells.reshape(full_width, quarter, lon_cells),
            "ch",
            split_axis=0,
            concat_axis=1,
            tiled=True,
        ),
        lax.all_to_all(
            conv_grad_cells.reshape(full_width, quarter, lon_cells),
            "ch",
            split_axis=0,
            concat_axis=1,
            tiled=True,
        ),
    )
    sum_in, sum_out = lax.psum((part_in, part_out), ("lon", "ch"))
    grad_weight_in = sum_in * grad_scale
    grad_weight_out = sum_out * grad_scale
    updated = (mask_f * (state_f + layer_scale[:, None, None] * branch.astype(jnp.float32))).astype(
        jnp.bfloat16
    )
    grad_rim = extended(grad_conv, (("lon", 2),), rim_width)
    padded_grad = jnp.pad(grad_rim.astype(jnp.float32), ((0, 0), (rim_width, rim_width), (0, 0)))
    grad_state = (grad_out + depth_back(padded_grad, kernel, row_count, lon_cells)).astype(
        jnp.bfloat16
    )
    return (updated, grad_state, grad_weight_in, grad_weight_out)


def solution(mesh):
    return jax.shard_map(
        body,
        mesh=mesh,
        in_specs=(
            P("ch", None, "lon"),
            P(None, "lon"),
            P("ch", None),
            P("ch"),
            P(),
            P(),
            P(),
            P(),
            P(),
            P(),
            P("ch"),
            P("ch", None, "lon"),
        ),
        out_specs=(P("ch", None, "lon"), P("ch", None, "lon"), P(), P()),
        check_vma=False,
    )
```

profile of v0, /device:TPU:1, one launch (start us, length us, event | category | flops | bytes accessed | tf_op | source)
XLA Modules:
  0.0 416.5 jit_solution(18222858004938454714)
XLA Ops:
  7.2 4.5 %fusion.192 = (bf16[100,64,3]{2,1,0:T(8,128)(2,1)}, bf16[100,64,3]{2,1,0:T(8,128)(2,1)}) fusion(bf16[100,64,128]{2,1,0:T(8,128)(2,1)} %param.12), kind=kLoop, calls=%fused_computation.345 | loop fusion | bytes 153600 | tf_op jit(solution)/shard_map/slice | solution.py:17
  19.7 7.5 %collective-permute-start.1 = (bf16[100,64,3]{0,1,2:T(8,128)(2,1)S(1)}, bf16[100,64,3]{0,1,2:T(8,128)(2,1)S(1)}, u32[]{:S(2)}, u32[]{:S(2)}) collective-permute-start(bf16[100,64,3]{0,1,2:T(8,128)(2,1)S(1)} %copy.41), channel_id=1, source_target_pairs={{4,0},{8,4},{12,8},{16,12},{20,16},{24,20},{28,24},{32,28},{36,32}... | collective-permute-start | bytes 115208 | tf_op jit(solution)/shard_map/ppermute | solution.py:22
  33.7 4.3 %maximum_convert_fusion = f32[100,64,134]{2,0,1:T(8,128)S(1)} fusion(bf16[100,64,3]{2,0,1:T(8,128)(2,1)} %copy.28, bf16[100,64,128]{2,0,1:T(8,128)(2,1)} %copy.23, bf16[100,64,3]{2,0,1:T(8,128)(2,1)} %copy.26), kind=kLoop, calls=%fused_computation.82 | loop fusion | flops 5145600 | bytes 5145600 | tf_op jit(solution)/shard_map/convert_element_type | solution.py:117
  38.1 40.2 %add_convert_fusion = bf16[100,64,128]{2,0,1:T(8,128)(2,1)} fusion(f32[100,64,134]{2,0,1:T(8,128)S(1)} %maximum_convert_fusion, f32[100]{0:T(128)} %param.15, f32[100]{0:T(128)} %get-tuple-element.66, f32[100]{0:T(128)} %get-tuple-element.67, f32[100]{0:T(128)S(1)} %get-tuple-element.20, f32[100]{0:T(128)S(1)} %get-tuple-element.21, ...), kind=kLoop, calls=%fused_computation.176 | loop fusion | flops 81100800 | bytes 32333840 | tf_op jit(solution)/shard_map/convert_element_type | solution.py:118
  78.3 25.5 %all_to_all.51 = bf16[100,64,128]{2,0,1:T(8,128)(2,1)S(1)} all-to-all(bf16[100,64,128]{2,0,1:T(8,128)(2,1)} %add_convert_fusion), channel_id=1, replica_groups=mesh['lon'=32,'ch'=4] {'ch'}, dimensions={1} | all-to-all | bytes 3276800 | tf_op jit(solution)/shard_map/all_to_all | solution.py:126
  104.4 10.9 %multiply_convert_fusion = (bf16[1600,2048]{1,0:T(8,128)(2,1)S(1)}, f32[2048,1600]{0,1:T(8,128)}) fusion(f32[1600]{0:T(1024)S(1)} %copy-done.23, bf16[400,1600]{1,0:T(8,128)(2,1)S(1)} %copy-done, f32[50,8,16,128]{3,2,1,0:T(8,128)S(1)} %bitcast.202, f32[400]{0:T(512)S(1)} %copy-done.25, f32[400]{0:T(512)S(1)} %copy-done.26, f32[2048]{0:T(1024)S(1)} %fusion.188, ...), kind=kOutput, calls=%fused_computation.10 | convolution fusion | flops 2658304000 | bytes 24243584 | tf_op jit(solution)/shard_map/dot_general | solution.py:78
  115.3 3.2 fusion.184
  120.2 5.5 %all-to-all-start.1 = ((bf16[400,16,128]{2,1,0:T(8,128)(2,1)}), bf16[400,16,128]{2,1,0:T(8,128)(2,1)}, u32[]{:S(2)}, u32[]{:S(2)}) async-start(bf16[400,16,128]{2,1,0:T(8,128)(2,1)} %bitcast.209), calls=%async_computation.1 | async-start | bytes 3276800 | tf_op jit(solution)/shard_map/all_to_all | solution.py:140
  125.7 20.0 %all-to-all-done.1 = bf16[400,16,128]{2,1,0:T(8,128)(2,1)} async-done(((bf16[400,16,128]{2,1,0:T(8,128)(2,1)}), bf16[400,16,128]{2,1,0:T(8,128)(2,1)}, u32[]{:S(2)}, u32[]{:S(2)}) %all-to-all-start.1) | async-done | bytes 1638432 | tf_op jit(solution)/shard_map/all_to_all | solution.py:140
  147.6 3.6 multiply_convert_fusion.1
  151.2 24.0 %all_to_all.52 = bf16[100,64,128]{2,0,1:T(8,128)(2,1)S(1)} all-to-all(bf16[100,64,128]{2,0,1:T(8,128)(2,1)S(1)} %get-tuple-element.17), channel_id=1, replica_groups=mesh['lon'=32,'ch'=4] {'ch'}, dimensions={1} | all-to-all | bytes 3276800 | tf_op jit(solution)/shard_map/all_to_all | solution.py:127
  175.5 14.4 %fusion.6 = bf16[1600,2048]{1,0:T(8,128)(2,1)S(1)} fusion(f32[2048,1600]{0,1:T(8,128)} %get-tuple-element.69, bf16[1600,400]{0,1:T(8,128)(2,1)S(1)} %copy-done.22, f32[1600]{0:T(1024)S(1)} %copy-done.23, bf16[50,8,16,128]{3,2,1,0:T(8,128)(2,1)S(1)} %bitcast.210), kind=kOutput, calls=%fused_computation.8 | convolution fusion | flops 2686976000 | bytes 22585600 | tf_op jit(solution)/shard_map/dot_general | solution.py:84
  189.9 5.6 %fusion.178 = (f32[2048]{0:T(1024)S(1)}, f32[2048,400]{0,1:T(8,128)}) fusion(f32[50,8,16,128]{3,2,1,0:T(8,128)S(1)} %bitcast.205, f32[2048]{0:T(1024)S(1)} %fusion.188, f32[2048]{0:T(1024)S(1)} %multiply_bitcast_fusion, f32[400]{0:T(512)S(1)} %copy-done.26, bf16[400,1600]{1,0:T(8,128)(2,1)S(1)} %copy-done, bf16[1600,2048]{1,0:T(8,128)(2,1)S(1)} %fusion.6), kind=kOutput, calls=%fused_computation.271 | convolution fusion | flops 2625533952 | bytes 14413376 | tf_op jit(solution)/shard_map/dot_general | solution.py:88
  197.6 4.8 %fusion.180 = bf16[50,8,16,128]{3,1,2,0:T(8,128)(2,1)S(1)} fusion(f32[50,8,16,128]{3,2,1,0:T(8,128)} %bitcast.203, f32[2048,400]{0,1:T(8,128)} %get-tuple-element.71, f32[2048]{0:T(1024)S(1)} %get-tuple-element.72, f32[2048]{0:T(1024)S(1)} %get-tuple-element.73, f32[2048]{0:T(1024)S(1)} %fusion.188, f32[2048]{0:T(1024)S(1)} %multiply_bitcast_fusion), kind=kLoop, calls=%fused_computation.278 | loop fusion | flops 5734400 | bytes 8224768
  204.0 5.4 %all-to-all-start.3 = ((bf16[400,16,128]{2,1,0:T(8,128)(2,1)}), bf16[400,16,128]{2,1,0:T(8,128)(2,1)}, u32[]{:S(2)}, u32[]{:S(2)}) async-start(bf16[400,16,128]{2,1,0:T(8,128)(2,1)} %bitcast.208), calls=%async_computation.3 | async-start | bytes 3276800 | tf_op jit(solution)/shard_map/all_to_all | solution.py:147
  211.2 9.2 %fusion.189 = f32[400,1600]{1,0:T(8,128)} fusion(bf16[1600,2048]{1,0:T(8,128)(2,1)} %copy-done.27, f32[50,8,16,128]{3,2,1,0:T(8,128)} %bitcast.204, f32[400]{0:T(512)S(1)} %copy-done.25, f32[400]{0:T(512)S(1)} %copy-done.26, f32[2048]{0:T(1024)S(1)} %fusion.188, f32[2048]{0:T(1024)S(1)} %multiply_bitcast_fusion), kind=kOutput, calls=%fused_computation.342 | convolution fusion | flops 2625536000 | bytes 12409984 | tf_op jit(solution)/shard_map/dot_general | solution.py:87
  220.4 9.0 %all-to-all-done.3 = bf16[400,16,128]{2,1,0:T(8,128)(2,1)} async-done(((bf16[400,16,128]{2,1,0:T(8,128)(2,1)}), bf16[400,16,128]{2,1,0:T(8,128)(2,1)}, u32[]{:S(2)}, u32[]{:S(2)}) %all-to-all-start.3) | async-done | bytes 1638432 | tf_op jit(solution)/shard_map/all_to_all | solution.py:147
  236.0 7.5 %collective-permute-start.3 = (bf16[100,64,3]{0,1,2:T(8,128)(2,1)S(1)}, bf16[100,64,3]{0,1,2:T(8,128)(2,1)S(1)}, u32[]{:S(2)}, u32[]{:S(2)}) collective-permute-start(bf16[100,64,3]{0,1,2:T(8,128)(2,1)S(1)} %copy.35), channel_id=1, source_target_pairs={{4,0},{8,4},{12,8},{16,12},{20,16},{24,20},{28,24},{32,28},{36,32}... | collective-permute-start | bytes 115208 | tf_op jit(solution)/shard_map/ppermute | solution.py:22
  243.5 8.0 %fusion.181 = f32[1600,400]{0,1:T(8,128)} fusion(bf16[1600,2048]{1,0:T(8,128)(2,1)} %copy-done.28, bf16[50,8,16,128]{3,2,1,0:T(8,128)(2,1)} %bitcast.211), kind=kOutput, calls=%fused_computation.279 | convolution fusion | flops 2621440000 | bytes 10752000 | tf_op jit(solution)/shard_map/dot_general | solution.py:86
  255.2 4.7 %maximum_convert_fusion.1 = f32[100,64,134]{2,0,1:T(8,128)S(1)} fusion(bf16[100,64,3]{2,0,1:T(8,128)(2,1)} %copy.37, bf16[100,64,128]{2,0,1:T(8,128)(2,1)} %bitcast.201, bf16[100,64,3]{2,0,1:T(8,128)(2,1)} %copy.36), kind=kLoop, calls=%fused_computation.83 | loop fusion | flops 5145600 | bytes 5145600 | tf_op jit(solution)/shard_map/convert_element_type | solution.py:162
  259.9 41.0 %fusion.173 = bf16[100,64,128]{2,0,1:T(8,128)(2,1)} fusion(f32[100,64,134]{2,0,1:T(8,128)S(1)} %maximum_convert_fusion.1, f32[100]{0:T(128)} %get-tuple-element.66, f32[100]{0:T(128)} %get-tuple-element.67, f32[100]{0:T(128)S(1)} %get-tuple-element.20, f32[100]{0:T(128)S(1)} %get-tuple-element.21, f32[100]{0:T(128)S(1)} %get-tuple-element.22, ...), kind=kLoop, calls=%fused_computation.263 | loop fusion | flops 82739200 | bytes 34003712 | tf_op jit(solution)/shard_map/convert_element_type | solution.py:163
  300.9 3.1 copy.39
  304.0 100.2 %all-reduce.5.cloned.1.call-done = (f32[400,1600]{1,0:T(8,128)}, f32[1600,400]{0,1:T(8,128)}) async-done(((f32[400,1600]{1,0:T(8,128)}, f32[1600,400]{0,1:T(8,128)}), (f32[400,1600]{1,0:T(8,128)}, f32[1600,400]{0,1:T(8,128)})) %all-reduce.5.cloned.1.call-update) | async-done | bytes 5120016 | tf_op jit(solution)/shard_map/psum | solution.py:155
  404.2 3.6 broadcast_multiply_fusion
  (92 shorter events, 36.3 us)
Async XLA Ops:
  7.2 97.1 %copy-start = (bf16[400,1600]{1,0:T(8,128)(2,1)S(1)}, bf16[400,1600]{1,0:T(8,128)(2,1)}, u32[]{:S(2)}) copy-start(bf16[400,1600]{1,0:T(8,128)(2,1)} %param.18) | copy-start | bytes 3840004
  7.2 20.6 %copy-start.2 = (bf16[100,64,128]{2,1,0:T(8,128)(2,1)S(1)}, bf16[100,64,128]{2,1,0:T(8,128)(2,1)}, u32[]{:S(2)}) copy-start(bf16[100,64,128]{2,1,0:T(8,128)(2,1)} %param.12) | copy-start | bytes 4915204
  7.2 19.9 %copy-start.11 = (f32[100,49]{0,1:T(8,128)S(1)}, f32[100,49]{0,1:T(8,128)}, u32[]{:S(2)}) copy-start(f32[100,49]{0,1:T(8,128)} %param.14) | copy-start | bytes 58804
  14.6 15.5 %collective-permute-start = (bf16[100,64,3]{0,1,2:T(8,128)(2,1)S(1)}, bf16[100,64,3]{0,1,2:T(8,128)(2,1)S(1)}, u32[]{:S(2)}, u32[]{:S(2)}) collective-permute-start(bf16[100,64,3]{0,1,2:T(8,128)(2,1)S(1)} %copy.40), channel_id=1, source_target_pairs={{0,4},{4,8},{8,12},{12,16},{16,20},{20,24},{24,28},{28,32},{32,36}... | collective-permute-start | bytes 115208 | tf_op jit(solution)/shard_map/ppermute | solution.py:20
  19.7 12.2 %collective-permute-start.1 = (bf16[100,64,3]{0,1,2:T(8,128)(2,1)S(1)}, bf16[100,64,3]{0,1,2:T(8,128)(2,1)S(1)}, u32[]{:S(2)}, u32[]{:S(2)}) collective-permute-start(bf16[100,64,3]{0,1,2:T(8,128)(2,1)S(1)} %copy.41), channel_id=1, source_target_pairs={{4,0},{8,4},{12,8},{16,12},{20,16},{24,20},{28,24},{32,28},{36,32}... | collective-permute-start | bytes 115208 | tf_op jit(solution)/shard_map/ppermute | solution.py:22
  27.2 10.8 %copy-start.12 = (f32[100]{0:T(128)}, f32[100]{0:T(128)S(1)}, u32[]{:S(2)}) copy-start(f32[100]{0:T(128)S(1)} %get-tuple-element.52) | copy-start | bytes 1204
  27.2 10.8 %copy-start.13 = (f32[100]{0:T(128)}, f32[100]{0:T(128)S(1)}, u32[]{:S(2)}) copy-start(f32[100]{0:T(128)S(1)} %get-tuple-element.53) | copy-start | bytes 1204
  27.2 10.8 %copy-start.14 = (f32[100]{0:T(128)}, f32[100]{0:T(128)S(1)}, u32[]{:S(2)}) copy-start(f32[100]{0:T(128)S(1)} %get-tuple-element.54) | copy-start | bytes 1204
  78.2 26.1 %copy-start.23 = (f32[1600]{0:T(1024)S(1)}, f32[1600]{0:T(1024)}, u32[]{:S(2)}) copy-start(f32[1600]{0:T(1024)} %param.19) | copy-start | bytes 19204
  78.2 26.1 %copy-start.25 = (f32[400]{0:T(512)S(1)}, f32[400]{0:T(512)}, u32[]{:S(2)}) copy-start(f32[400]{0:T(512)} %param.17) | copy-start | bytes 4804
  78.3 26.1 %copy-start.26 = (f32[400]{0:T(512)S(1)}, f32[400]{0:T(512)}, u32[]{:S(2)}) copy-start(f32[400]{0:T(512)} %param.16) | copy-start | bytes 4804
  104.3 11.0 %copy-start.4 = (f32[100,4,16,128]{3,2,0,1:T(8,128)}, f32[100,4,16,128]{3,2,0,1:T(8,128)S(1)}, u32[]{:S(2)}) copy-start(f32[100,4,16,128]{3,2,0,1:T(8,128)S(1)} %get-tuple-element.12) | copy-start | bytes 9830404
  104.3 11.0 %copy-start.21 = (bf16[1600,400]{0,1:T(8,128)(2,1)S(1)}, bf16[1600,400]{0,1:T(8,128)(2,1)}, u32[]{:S(2)}) copy-start(bf16[1600,400]{0,1:T(8,128)(2,1)} %param.20) | copy-start | bytes 3840004
  104.3 11.0 %copy-start.24 = (f32[400]{0:T(512)S(1)}, f32[400]{0:T(512)}, u32[]{:S(2)}) copy-start(f32[400]{0:T(512)} %param.21) | copy-start | bytes 4804
  120.2 27.4 %copy-start.3 = (bf16[100,64,128]{2,1,0:T(8,128)(2,1)S(1)}, bf16[100,64,128]{2,1,0:T(8,128)(2,1)}, u32[]{:S(2)}) copy-start(bf16[100,64,128]{2,1,0:T(8,128)(2,1)} %param.12) | copy-start | bytes 4915204
  120.2 27.4 %copy-start.20 = (f32[100]{0:T(128)S(1)}, f32[100]{0:T(128)}, u32[]{:S(2)}) copy-start(f32[100]{0:T(128)} %param.22) | copy-start | bytes 1204
  120.2 25.5 %all-to-all-start.1 = ((bf16[400,16,128]{2,1,0:T(8,128)(2,1)}), bf16[400,16,128]{2,1,0:T(8,128)(2,1)}, u32[]{:S(2)}, u32[]{:S(2)}) async-start(bf16[400,16,128]{2,1,0:T(8,128)(2,1)} %bitcast.209), calls=%async_computation.1 | async-start | bytes 3276800 | tf_op jit(solution)/shard_map/all_to_all | solution.py:140
  151.2 24.3 %copy-start.22 = (bf16[1600,400]{0,1:T(8,128)(2,1)S(1)}, bf16[1600,400]{0,1:T(8,128)(2,1)}, u32[]{:S(2)}) copy-start(bf16[1600,400]{0,1:T(8,128)(2,1)} %param.20) | copy-start | bytes 3840004
  175.5 14.4 %copy-start.9 = (bf16[100,4,16,128]{3,2,0,1:T(8,128)(2,1)}, bf16[100,4,16,128]{3,2,0,1:T(8,128)(2,1)S(1)}, u32[]{:S(2)}) copy-start(bf16[100,4,16,128]{3,2,0,1:T(8,128)(2,1)S(1)} %copy.32) | copy-start | bytes 4915204
  175.5 14.4 %copy-start.5 = (f32[100,4,16,128]{3,2,0,1:T(8,128)S(1)}, f32[100,4,16,128]{3,2,0,1:T(8,128)}, u32[]{:S(2)}) copy-start(f32[100,4,16,128]{3,2,0,1:T(8,128)} %copy-done.4) | copy-start | bytes 9830404
  204.0 25.4 %all-to-all-start.3 = ((bf16[400,16,128]{2,1,0:T(8,128)(2,1)}), bf16[400,16,128]{2,1,0:T(8,128)(2,1)}, u32[]{:S(2)}, u32[]{:S(2)}) async-start(bf16[400,16,128]{2,1,0:T(8,128)(2,1)} %bitcast.208), calls=%async_computation.3 | async-start | bytes 3276800 | tf_op jit(solution)/shard_map/all_to_all | solution.py:147
  209.4 194.8 %all-reduce.5.cloned.1.call-start = ((), (), s32[]{:S(2)}) async-start(), calls=%async_computation.4 | async-start | bytes 10649600 | tf_op jit(solution)/shard_map/psum | solution.py:155
  235.0 16.5 %collective-permute-start.2 = (bf16[100,64,3]{0,1,2:T(8,128)(2,1)S(1)}, bf16[100,64,3]{0,1,2:T(8,128)(2,1)S(1)}, u32[]{:S(2)}, u32[]{:S(2)}) collective-permute-start(bf16[100,64,3]{0,1,2:T(8,128)(2,1)S(1)} %copy.34), channel_id=1, source_target_pairs={{0,4},{4,8},{8,12},{12,16},{16,20},{20,24},{24,28},{28,32},{32,36}... | collective-permute-start | bytes 115208 | tf_op jit(solution)/shard_map/ppermute | solution.py:20
  236.0 17.3 %collective-permute-start.3 = (bf16[100,64,3]{0,1,2:T(8,128)(2,1)S(1)}, bf16[100,64,3]{0,1,2:T(8,128)(2,1)S(1)}, u32[]{:S(2)}, u32[]{:S(2)}) collective-permute-start(bf16[100,64,3]{0,1,2:T(8,128)(2,1)S(1)} %copy.35), channel_id=1, source_target_pairs={{4,0},{8,4},{12,8},{16,12},{20,16},{24,20},{28,24},{32,28},{36,32}... | collective-permute-start | bytes 115208 | tf_op jit(solution)/shard_map/ppermute | solution.py:22
  (12 other events, 82.7 us)
Sparse Core Ops, SparseCore 0:
  251.6 152.4 all-reduce.4
where the time goes:
time: 424 us; the launch traced here: 417 us
  waiting for transfers between devices  129 us (30%)
  other arithmetic  106 us (25%)
  matrix products  51.3 us (12%)
  blocking collectives  49.6 us (12%)
  local copies, waits for them, and re-layouts  37 us (9%)
  starting transfers between devices  28.3 us (7%)
  between operations  14.7 us (3%)
    psum x1, waiting for transfers between devices, body(): sum_in, sum_out = lax.psum((part_in, part_out), ('lon', 'ch'))  100 us
    convert_element_type x1, other arithmetic, body(): (grad_out + depth_back(padded_grad, kernel, row_count, lon_cells)).astype...  41 us
    convert_element_type x1, other arithmetic, body(): (depth_taps(padded, kernel, row_count, lon_cells) + conv_bias[:, None, No...  40.2 us
    all_to_all x1, blocking collectives, body(): lax.all_to_all(conv_out, 'ch', split_axis=1, concat_axis=0, tiled=True)  25.5 us
    all_to_all x1, blocking collectives, body(): lax.all_to_all(grad_branch, 'ch', split_axis=1, concat_axis=0, tiled=True)  24 us
    all_to_all x1, waiting for transfers between devices, body(): lax.all_to_all(branch_cells.reshape(full_width, quarter, lon_cells), 'ch'...  20 us
    unnamed x65, local copies, waits for them, and re-layouts  16.1 us
    ppermute x2, starting transfers between devices, extended(): lax.ppermute(head, axis, [((i + 1) % count, i) for i in range(count)])  15 us
  transfers between devices with their start and end apart: 7, of which 3 were waited for; matrix products, arithmetic and copies ran while one was open for 19% of the time, Pallas kernels for 0%

commit v1 on v0

--- a/solution.py
+++ b/solution.py
@@ -152,7 +152,7 @@
             tiled=True,
         ),
     )
-    sum_in, sum_out = lax.psum((part_in, part_out), ("lon", "ch"))
+    sum_in, sum_out = lax.psum(lax.psum((part_in, part_out), "ch"), "lon")
     grad_weight_in = sum_in * grad_scale
     grad_weight_out = sum_out * grad_scale
     updated = (mask_f * (state_f + layer_scale[:, None, None] * branch.astype(jnp.float32))).astype(

time: 424 us -> 724 us (1.71)
  the two profiles are of different devices: /device:TPU:1 before, /device:TPU:0 now
where the time goes in v1:
time: 724 us; the launch traced here: 717 us
  waiting for transfers between devices  433 us (60%)
  other arithmetic  106 us (15%)
  blocking collectives  49.7 us (7%)
  matrix products  47.5 us (7%)
  local copies, waits for them, and re-layouts  40 us (6%)
  starting transfers between devices  25.2 us (3%)
  between operations  14.8 us (2%)
    psum x2, waiting for transfers between devices, body(): sum_in, sum_out = lax.psum(lax.psum((part_in, part_out), 'ch'), 'lon')  412 us
    convert_element_type x1, other arithmetic, body(): (grad_out + depth_back(padded_grad, kernel, row_count, lon_cells)).astype...  41 us
    convert_element_type x1, other arithmetic, body(): (depth_taps(padded, kernel, row_count, lon_cells) + conv_bias[:, None, No...  40.2 us
    all_to_all x1, blocking collectives, body(): lax.all_to_all(conv_out, 'ch', split_axis=1, concat_axis=0, tiled=True)  25.6 us
    all_to_all x1, blocking collectives, body(): lax.all_to_all(grad_branch, 'ch', split_axis=1, concat_axis=0, tiled=True)  24.1 us
    all_to_all x1, waiting for transfers between devices, body(): lax.all_to_all(branch_cells.reshape(full_width, quarter, lon_cells), 'ch'...  20.8 us
    unnamed x67, local copies, waits for them, and re-layouts  18.8 us
  transfers between devices with their start and end apart: 8, of which 3 were waited for; matrix products, arithmetic and copies ran while one was open for 12% of the time, Pallas kernels for 0%

profile of v1, /device:TPU:0, one launch (start us, length us, event | category | flops | bytes accessed | tf_op | source)
XLA Modules:
  0.0 716.6 jit_solution(470799908180663181)
XLA Ops:
  7.2 4.5 fusion.192
  19.2 7.5 %collective-permute-start.1 = (bf16[100,64,3]{0,1,2:T(8,128)(2,1)S(1)}, bf16[100,64,3]{0,1,2:T(8,128)(2,1)S(1)}, u32[]{:S(2)}, u32[]{:S(2)}) collective-permute-start(bf16[100,64,3]{0,1,2:T(8,128)(2,1)S(1)} %copy.41), channel_id=1, source_target_pairs={{4,0},{8,4},{12,8},{16,12},{20,16},{24,20},{28,24},{32,28},{36,32}... | collective-permute-start | bytes 115208 | tf_op jit(solution)/shard_map/ppermute | solution.py:22
  33.2 4.3 maximum_convert_fusion
  37.6 40.2 %add_convert_fusion = bf16[100,64,128]{2,0,1:T(8,128)(2,1)} fusion(f32[100,64,134]{2,0,1:T(8,128)S(1)} %maximum_convert_fusion, f32[100]{0:T(128)} %param.15, f32[100]{0:T(128)} %get-tuple-element.68, f32[100]{0:T(128)} %get-tuple-element.69, f32[100]{0:T(128)S(1)} %get-tuple-element.22, f32[100]{0:T(128)S(1)} %get-tuple-element.23, ...), kind=kLoop, calls=%fused_computation.176 | loop fusion | flops 81100800 | bytes 32333840 | tf_op jit(solution)/shard_map/convert_element_type | solution.py:118
  77.8 25.6 %all_to_all.51 = bf16[100,64,128]{2,0,1:T(8,128)(2,1)S(1)} all-to-all(bf16[100,64,128]{2,0,1:T(8,128)(2,1)} %add_convert_fusion), channel_id=1, replica_groups=mesh['lon'=32,'ch'=4] {'ch'}, dimensions={1} | all-to-all | bytes 3276800 | tf_op jit(solution)/shard_map/all_to_all | solution.py:126
  104.0 11.0 %multiply_convert_fusion = (bf16[1600,2048]{1,0:T(8,128)(2,1)S(1)}, f32[2048,1600]{0,1:T(8,128)}) fusion(f32[1600]{0:T(1024)S(1)} %copy-done.22, bf16[400,1600]{1,0:T(8,128)(2,1)S(1)} %copy-done, f32[50,8,16,128]{3,2,1,0:T(8,128)S(1)} %bitcast.202, f32[400]{0:T(512)S(1)} %copy-done.24, f32[400]{0:T(512)S(1)} %copy-done.25, f32[2048]{0:T(1024)S(1)} %fusion.188, ...), kind=kOutput, calls=%fused_computation.10 | convolution fusion | flops 2658304000 | bytes 24243584 | tf_op jit(solution)/shard_map/dot_general | solution.py:78
  115.0 3.2 fusion.184
  119.9 4.5 all-to-all-start.1
  124.5 20.8 %all-to-all-done.1 = bf16[400,16,128]{2,1,0:T(8,128)(2,1)} async-done(((bf16[400,16,128]{2,1,0:T(8,128)(2,1)}), bf16[400,16,128]{2,1,0:T(8,128)(2,1)}, u32[]{:S(2)}, u32[]{:S(2)}) %all-to-all-start.1) | async-done | bytes 1638432 | tf_op jit(solution)/shard_map/all_to_all | solution.py:140
  147.2 3.6 multiply_convert_fusion.1
  150.8 24.1 %all_to_all.52 = bf16[100,64,128]{2,0,1:T(8,128)(2,1)S(1)} all-to-all(bf16[100,64,128]{2,0,1:T(8,128)(2,1)S(1)} %get-tuple-element.19), channel_id=1, replica_groups=mesh['lon'=32,'ch'=4] {'ch'}, dimensions={1} | all-to-all | bytes 3276800 | tf_op jit(solution)/shard_map/all_to_all | solution.py:127
  175.2 4.7 fusion.181
  179.9 13.9 %fusion.6 = bf16[1600,2048]{1,0:T(8,128)(2,1)S(1)} fusion(f32[2048,1600]{0,1:T(8,128)} %get-tuple-element.71, bf16[1600,400]{0,1:T(8,128)(2,1)S(1)} %copy-done.21, f32[1600]{0:T(1024)S(1)} %copy-done.22, bf16[50,8,16,128]{3,2,1,0:T(8,128)(2,1)S(1)} %bitcast.212), kind=kOutput, calls=%fused_computation.8 | convolution fusion | flops 2686976000 | bytes 22585600 | tf_op jit(solution)/shard_map/dot_general | solution.py:84
  196.5 5.5 fusion.189
  202.1 9.2 %fusion.178 = (f32[2048]{0:T(1024)S(1)}, f32[2048,400]{0,1:T(8,128)}) fusion(f32[50,8,16,128]{3,2,1,0:T(8,128)} %bitcast.203, f32[2048]{0:T(1024)S(1)} %fusion.188, f32[2048]{0:T(1024)S(1)} %multiply_bitcast_fusion, f32[400]{0:T(512)S(1)} %copy-done.25, bf16[400,1600]{1,0:T(8,128)(2,1)S(1)} %copy-done, bf16[1600,2048]{1,0:T(8,128)(2,1)} %copy-done.26), kind=kOutput, calls=%fused_computation.271 | convolution fusion | flops 2625533952 | bytes 14413376 | tf_op jit(solution)/shard_map/dot_general | solution.py:88
  213.4 4.8 fusion.180
  219.8 3.6 all-to-all-start.3
  223.5 104.6 %all-reduce.9.cloned.1.call-done = (f32[400,1600]{1,0:T(8,128)}, f32[1600,400]{0,1:T(8,128)}) async-done(((f32[400,1600]{1,0:T(8,128)}, f32[1600,400]{0,1:T(8,128)}), (f32[400,1600]{1,0:T(8,128)}, f32[1600,400]{0,1:T(8,128)})) %all-reduce.9.cloned.1.call-update) | async-done | bytes 5120016 | tf_op jit(solution)/shard_map/psum | solution.py:155
  336.4 6.3 collective-permute-start.3
  348.0 4.3 maximum_convert_fusion.1
  352.3 41.0 %fusion.173 = bf16[100,64,128]{2,0,1:T(8,128)(2,1)} fusion(f32[100,64,134]{2,0,1:T(8,128)S(1)} %maximum_convert_fusion.1, f32[100]{0:T(128)} %get-tuple-element.68, f32[100]{0:T(128)} %get-tuple-element.69, f32[100]{0:T(128)S(1)} %get-tuple-element.22, f32[100]{0:T(128)S(1)} %get-tuple-element.23, f32[100]{0:T(128)S(1)} %get-tuple-element.24, ...), kind=kLoop, calls=%fused_computation.263 | loop fusion | flops 82739200 | bytes 34003712 | tf_op jit(solution)/shard_map/convert_element_type | solution.py:163
  393.3 3.1 copy.39
  396.3 307.9 %all-reduce.7.cloned.1.call-done = (f32[400,1600]{1,0:T(8,128)}, f32[1600,400]{0,1:T(8,128)}) async-done(((f32[400,1600]{1,0:T(8,128)}, f32[1600,400]{0,1:T(8,128)}), (f32[400,1600]{1,0:T(8,128)}, f32[1600,400]{0,1:T(8,128)})) %all-reduce.7.cloned.1.call-update) | async-done | bytes 5120016 | tf_op jit(solution)/shard_map/psum | solution.py:155
  704.2 3.6 broadcast_multiply_fusion
  (98 shorter events, 40.1 us)
Async XLA Ops:
  7.2 96.8 %copy-start = (bf16[400,1600]{1,0:T(8,128)(2,1)S(1)}, bf16[400,1600]{1,0:T(8,128)(2,1)}, u32[]{:S(2)}) copy-start(bf16[400,1600]{1,0:T(8,128)(2,1)} %param.18) | copy-start | bytes 3840004
  7.2 20.2 %copy-start.2 = (bf16[100,64,128]{2,1,0:T(8,128)(2,1)S(1)}, bf16[100,64,128]{2,1,0:T(8,128)(2,1)}, u32[]{:S(2)}) copy-start(bf16[100,64,128]{2,1,0:T(8,128)(2,1)} %param.12) | copy-start | bytes 4915204
  7.2 19.5 %copy-start.10 = (f32[100,49]{0,1:T(8,128)S(1)}, f32[100,49]{0,1:T(8,128)}, u32[]{:S(2)}) copy-start(f32[100,49]{0,1:T(8,128)} %param.14) | copy-start | bytes 58804
  14.6 15.1 %collective-permute-start = (bf16[100,64,3]{0,1,2:T(8,128)(2,1)S(1)}, bf16[100,64,3]{0,1,2:T(8,128)(2,1)S(1)}, u32[]{:S(2)}, u32[]{:S(2)}) collective-permute-start(bf16[100,64,3]{0,1,2:T(8,128)(2,1)S(1)} %copy.40), channel_id=1, source_target_pairs={{0,4},{4,8},{8,12},{12,16},{16,20},{20,24},{24,28},{28,32},{32,36}... | collective-permute-start | bytes 115208 | tf_op jit(solution)/shard_map/ppermute | solution.py:20
  19.2 12.3 %collective-permute-start.1 = (bf16[100,64,3]{0,1,2:T(8,128)(2,1)S(1)}, bf16[100,64,3]{0,1,2:T(8,128)(2,1)S(1)}, u32[]{:S(2)}, u32[]{:S(2)}) collective-permute-start(bf16[100,64,3]{0,1,2:T(8,128)(2,1)S(1)} %copy.41), channel_id=1, source_target_pairs={{4,0},{8,4},{12,8},{16,12},{20,16},{24,20},{28,24},{32,28},{36,32}... | collective-permute-start | bytes 115208 | tf_op jit(solution)/shard_map/ppermute | solution.py:22
  26.7 10.8 %copy-start.11 = (f32[100]{0:T(128)}, f32[100]{0:T(128)S(1)}, u32[]{:S(2)}) copy-start(f32[100]{0:T(128)S(1)} %get-tuple-element.54) | copy-start | bytes 1204
  77.8 26.2 %copy-start.22 = (f32[1600]{0:T(1024)S(1)}, f32[1600]{0:T(1024)}, u32[]{:S(2)}) copy-start(f32[1600]{0:T(1024)} %param.19) | copy-start | bytes 19204
  77.8 26.2 %copy-start.24 = (f32[400]{0:T(512)S(1)}, f32[400]{0:T(512)}, u32[]{:S(2)}) copy-start(f32[400]{0:T(512)} %param.17) | copy-start | bytes 4804
  77.8 26.2 %copy-start.25 = (f32[400]{0:T(512)S(1)}, f32[400]{0:T(512)}, u32[]{:S(2)}) copy-start(f32[400]{0:T(512)} %param.16) | copy-start | bytes 4804
  103.9 11.1 %copy-start.4 = (f32[100,4,16,128]{3,2,0,1:T(8,128)}, f32[100,4,16,128]{3,2,0,1:T(8,128)S(1)}, u32[]{:S(2)}) copy-start(f32[100,4,16,128]{3,2,0,1:T(8,128)S(1)} %get-tuple-element.14) | copy-start | bytes 9830404
  104.0 11.0 %copy-start.20 = (bf16[1600,400]{0,1:T(8,128)(2,1)S(1)}, bf16[1600,400]{0,1:T(8,128)(2,1)}, u32[]{:S(2)}) copy-start(bf16[1600,400]{0,1:T(8,128)(2,1)} %param.20) | copy-start | bytes 3840004
  104.0 11.0 %copy-start.23 = (f32[400]{0:T(512)S(1)}, f32[400]{0:T(512)}, u32[]{:S(2)}) copy-start(f32[400]{0:T(512)} %param.21) | copy-start | bytes 4804
  119.9 27.3 %copy-start.3 = (bf16[100,64,128]{2,1,0:T(8,128)(2,1)S(1)}, bf16[100,64,128]{2,1,0:T(8,128)(2,1)}, u32[]{:S(2)}) copy-start(bf16[100,64,128]{2,1,0:T(8,128)(2,1)} %param.12) | copy-start | bytes 4915204
  119.9 27.3 %copy-start.19 = (f32[100]{0:T(128)S(1)}, f32[100]{0:T(128)}, u32[]{:S(2)}) copy-start(f32[100]{0:T(128)} %param.22) | copy-start | bytes 1204
  119.9 25.4 %all-to-all-start.1 = ((bf16[400,16,128]{2,1,0:T(8,128)(2,1)}), bf16[400,16,128]{2,1,0:T(8,128)(2,1)}, u32[]{:S(2)}, u32[]{:S(2)}) async-start(bf16[400,16,128]{2,1,0:T(8,128)(2,1)} %bitcast.210), calls=%async_computation.1 | async-start | bytes 3276800 | tf_op jit(solution)/shard_map/all_to_all | solution.py:140
  124.4 203.6 %all-reduce.9.cloned.1.call-start = ((), (), s32[]{:S(2)}) async-start(), calls=%async_computation.5 | async-start | bytes 10649600 | tf_op jit(solution)/shard_map/psum | solution.py:155
  145.3 29.9 %slice-start = ((s8[6553600]{0:T(1024)(128)(4,1)}), s8[4194304]{0:T(1024)(128)(4,1)S(1)}, s32[]{:S(2)}) async-start(s8[6553600]{0:T(1024)(128)(4,1)} %bitcast.213), calls=%async_computation.6 | async-start | bytes 8388608
  147.2 28.0 %slice-start.1 = ((s8[6553600]{0:T(1024)(128)(4,1)}), s8[2359296]{0:T(1024)(128)(4,1)S(1)}, s32[]{:S(2)}) async-start(s8[6553600]{0:T(1024)(128)(4,1)} %bitcast.213), calls=%async_computation.7 | async-start | bytes 4718592
  179.9 16.7 %copy-start.5 = (f32[100,4,16,128]{3,2,0,1:T(8,128)S(1)}, f32[100,4,16,128]{3,2,0,1:T(8,128)}, u32[]{:S(2)}) copy-start(f32[100,4,16,128]{3,2,0,1:T(8,128)} %copy-done.4) | copy-start | bytes 9830404
  219.8 108.3 %all-to-all-start.3 = ((bf16[400,16,128]{2,1,0:T(8,128)(2,1)}), bf16[400,16,128]{2,1,0:T(8,128)(2,1)S(1)}, u32[]{:S(2)}, u32[]{:S(2)}) async-start(bf16[400,16,128]{2,1,0:T(8,128)(2,1)} %bitcast.209), calls=%async_computation.3 | async-start | bytes 3276800 | tf_op jit(solution)/shard_map/all_to_all | solution.py:147
  223.4 480.8 %all-reduce.7.cloned.1.call-start = ((), (), s32[]{:S(2)}) async-start(), calls=%async_computation.4 | async-start | bytes 10649600 | tf_op jit(solution)/shard_map/psum | solution.py:155
  330.9 11.9 %copy-start.6 = (bf16[100,64,128]{2,0,1:T(8,128)(2,1)S(1)}, bf16[100,64,128]{2,0,1:T(8,128)(2,1)}, u32[]{:S(2)}) copy-start(bf16[100,64,128]{2,0,1:T(8,128)(2,1)} %get-tuple-element.20) | copy-start | bytes 4915204
  333.0 11.4 %collective-permute-start.2 = (bf16[100,64,3]{0,1,2:T(8,128)(2,1)S(1)}, bf16[100,64,3]{0,1,2:T(8,128)(2,1)S(1)}, u32[]{:S(2)}, u32[]{:S(2)}) collective-permute-start(bf16[100,64,3]{0,1,2:T(8,128)(2,1)S(1)} %copy.34), channel_id=1, source_target_pairs={{0,4},{4,8},{8,12},{12,16},{16,20},{20,24},{24,28},{28,32},{32,36}... | collective-permute-start | bytes 115208 | tf_op jit(solution)/shard_map/ppermute | solution.py:20
  336.4 9.7 %collective-permute-start.3 = (bf16[100,64,3]{0,1,2:T(8,128)(2,1)S(1)}, bf16[100,64,3]{0,1,2:T(8,128)(2,1)S(1)}, u32[]{:S(2)}, u32[]{:S(2)}) collective-permute-start(bf16[100,64,3]{0,1,2:T(8,128)(2,1)S(1)} %copy.35), channel_id=1, source_target_pairs={{4,0},{8,4},{12,8},{16,12},{20,16},{24,20},{28,24},{32,28},{36,32}... | collective-permute-start | bytes 115208 | tf_op jit(solution)/shard_map/ppermute | solution.py:22
  (14 other events, 98.8 us)
Sparse Core Ops, SparseCore 0:
  202.2 125.8 all-reduce.8
  330.7 373.5 all-reduce.6
